TPU v7x, 256 devices: a whole 4x4x8 slice. The times are simulated.
256 devices in a mesh: wide: 32 (over x, z), blk: 8 (over y, core).
Axes of the slice: x: 4, y: 4, z: 8, core: 2. Of those that a mesh axis runs over, the one named last changes fastest.
Arguments:
- amplitudes: bfloat16 [32, 32, 32, 4096], P('blk', 'wide'), may hold values from -6 to 6
- integrals: bfloat16 [32, 2, 2048, 4096], P('wide', None, 'blk'), may hold values from -0.09375 to 0.09375
- owner: int32 [32], replicated, may hold values from 0 to 31, each once
- targets: int32 [32, 2], replicated, may hold values from 0 to 31, all different within a row
- counts: int32 [32], replicated, may hold values from 1 to 2, 48 in all
Outputs:
- ladder: bfloat16 [32, 32, 32, 2048], P(None, 'blk', 'wide')
Inputs may be any that keep to these rules, and one draw needn't show every extreme that they name: Each contracted tile has its own owner slot. `targets`: the output tiles of one contracted tile are distinct, and every output tile is named by some contracted tile. The counts sum to 48 and one of them is 2.
All inputs are finite; a program needn't handle non-finite values.
Results may differ from a plain program's by a relative error of at most 0.0044.
Values may be sent and summed in bfloat16 or wider, within the bound.
A program may use at most 128 MiB of HBM per device.

v0:
```python
import jax
import jax.numpy as jnp
from jax import lax
from jax.sharding import PartitionSpec as P


def body(amplitudes, integrals, owner, targets, counts):
    wide_count = lax.axis_size("wide")
    my_index = lax.axis_index("wide")
    tile_ids = jnp.arange(owner.shape[0], dtype=jnp.int32)
    holder = jnp.sum(jnp.where(owner[None, :] == tile_ids[:, None], tile_ids[None, :], 0), axis=1)
    ordered = jnp.take(amplitudes, holder, axis=2)
    my_tile = lax.all_to_all(ordered, "wide", split_axis=2, concat_axis=1, tiled=True)
    my_holder = lax.dynamic_index_in_dim(holder, my_index, 0, keepdims=False)
    my_count = lax.dynamic_index_in_dim(counts, my_holder, 0, keepdims=False)
    slot_ids = jnp.arange(targets.shape[1], dtype=jnp.int32)
    live_slots = (slot_ids < my_count).astype(jnp.float32)
    my_integrals = integrals[0]
    width = my_tile.shape[3]
    pair_rows = my_tile.reshape(-1, width)
    partial_value = jnp.einsum(
        "rc,kac->rka",
        pair_rows,
        lax.all_gather(my_integrals, "blk", axis=1, tiled=True),
        preferred_element_type=jnp.float32,
    )
    shaped = (partial_value * live_slots[None, :, None]).astype(jnp.bfloat16)
    shaped = shaped.reshape(my_tile.shape[0], my_tile.shape[1], targets.shape[1], shaped.shape[2])
    received = lax.all_to_all(shaped, "wide", split_axis=1, concat_axis=2, tiled=True)
    slot_targets = jnp.take(targets, holder, axis=0).reshape(-1)
    window_ids = jnp.arange(wide_count, dtype=jnp.int32)
    selector = (slot_targets[None, :] == window_ids[:, None]).astype(jnp.bfloat16)
    ladder = jnp.einsum("ps,ijsa->pija", selector, received, preferred_element_type=jnp.float32)
    return ladder.astype(jnp.bfloat16)


def solution(mesh):
    placed = (P("blk", "wide", None, None), P("wide", None, "blk", None), P(), P(), P())
    return jax.shard_map(
        body, mesh=mesh, in_specs=placed, out_specs=P(None, "blk", "wide", None), check_vma=False
    )
```

profile of v0, /device:TPU:8, one launch (start us, length us, event | category | flops | bytes accessed | tf_op | source)
XLA Modules:
  0.0 236.6 jit_solution(17188635275053602947)
XLA Ops:
  6.5 0.0 copy-start
  6.5 0.0 all-gather.3.cloned.1.call-start
  6.5 0.7 all-gather.3.cloned.1.call-update
  7.3 2.0 copy.32
  9.3 0.8 select_reduce_fusion
  10.1 1.4 gather_fusion.1
  11.6 1.5 fusion.9
  13.1 11.3 %all-to-all-start = ((bf16[4,1,32,4096]{3,0,1,2:T(4,128)(2,1)}), bf16[4,1,32,4096]{3,0,1,2:T(4,128)(2,1)S(1)}, u32[]{:S(2)}, u32[]{:S(2)}) async-start(bf16[4,1,32,4096]{3,0,1,2:T(4,128)(2,1)} %fusion.9), calls=%async_computation | async-start | bytes 2097152 | tf_op jit(solution)/shard_map/all_to_all | solution.py:13
  24.4 0.6 dynamic_slice.7
  27.0 1.3 dynamic_slice.8
  28.2 0.7 compare_convert_fusion
  28.9 24.1 %all-to-all-done = bf16[4,1,32,4096]{3,0,1,2:T(4,128)(2,1)S(1)} async-done(((bf16[4,1,32,4096]{3,0,1,2:T(4,128)(2,1)}), bf16[4,1,32,4096]{3,0,1,2:T(4,128)(2,1)S(1)}, u32[]{:S(2)}, u32[]{:S(2)}) %all-to-all-start) | async-done | bytes 1048608 | tf_op jit(solution)/shard_map/all_to_all | solution.py:13
  53.0 0.6 copy.24
  53.6 116.9 %all-gather.3.cloned.1.call-done = bf16[1,2,2048,4096]{3,2,1,0:T(8,128)(2,1)} async-done(((bf16[1,2,256,4096]{3,2,1,0:T(8,128)(2,1)}), bf16[1,2,2048,4096]{3,2,1,0:T(8,128)(2,1)}) %all-gather.3.cloned.1.call-update) | async-done | bytes 33554448 | tf_op jit(solution)/shard_map/all_gather | solution.py:24
  170.5 16.0 %fusion.5 = bf16[128,2,2048]{2,0,1:T(8,128)(2,1)S(1)} fusion(bf16[128,4096,1]{1,0,2:T(8,128)(2,1)S(1)} %bitcast.36, bf16[1,2,2048,4096]{3,2,1,0:T(8,128)(2,1)} %all-gather.3.cloned.1.call-done, f32[2]{0:T(128)S(1)} %compare_convert_fusion), kind=kOutput, calls=%fused_computation.6 | convolution fusion | flops 4296015872 | bytes 35651592 | tf_op jit(solution)/shard_map/rc,kac->rka/dot_general | solution.py:21
  186.6 1.8 copy.25
  188.3 9.8 %all-to-all-start.1 = ((bf16[4,32,2,2048]{3,0,2,1:T(4,128)(2,1)}), bf16[4,32,2,2048]{3,0,2,1:T(4,128)(2,1)S(1)}, u32[]{:S(2)}, u32[]{:S(2)}) async-start(bf16[4,32,2,2048]{3,0,2,1:T(4,128)(2,1)} %copy.25), calls=%async_computation.1 | async-start | bytes 2097152 | tf_op jit(solution)/shard_map/all_to_all | solution.py:29
  198.2 0.0 copy-done
  198.2 0.1 copy.21
  198.3 0.6 gather_fusion
  198.9 0.1 broadcast_select_fusion
  198.9 0.1 select_n.56
  199.0 28.2 %all-to-all-done.1 = bf16[4,32,2,2048]{3,0,2,1:T(4,128)(2,1)S(1)} async-done(((bf16[4,32,2,2048]{3,0,2,1:T(4,128)(2,1)}), bf16[4,32,2,2048]{3,0,2,1:T(4,128)(2,1)S(1)}, u32[]{:S(2)}, u32[]{:S(2)}) %all-to-all-start.1) | async-done | bytes 1048608 | tf_op jit(solution)/shard_map/all_to_all | solution.py:29
  227.2 1.3 fusion.8
  228.5 1.2 copy.27
  (3 shorter events, 0.0 us)
Async XLA Ops:
  6.5 191.7 %copy-start = (s32[32,2]{0,1:T(2,128)S(1)}, s32[32,2]{0,1:T(2,128)}, u32[]{:S(2)}) copy-start(s32[32,2]{0,1:T(2,128)} %param.8) | copy-start | bytes 772
  6.5 164.0 %all-gather.3.cloned.1.call-start = ((), (), s32[]{:S(2)}) async-start(), calls=%async_computation.2 | async-start | bytes 37748736 | tf_op jit(solution)/shard_map/all_gather | solution.py:24
  13.1 39.9 %all-to-all-start = ((bf16[4,1,32,4096]{3,0,1,2:T(4,128)(2,1)}), bf16[4,1,32,4096]{3,0,1,2:T(4,128)(2,1)S(1)}, u32[]{:S(2)}, u32[]{:S(2)}) async-start(bf16[4,1,32,4096]{3,0,1,2:T(4,128)(2,1)} %fusion.9), calls=%async_computation | async-start | bytes 2097152 | tf_op jit(solution)/shard_map/all_to_all | solution.py:13
  188.3 38.9 %all-to-all-start.1 = ((bf16[4,32,2,2048]{3,0,2,1:T(4,128)(2,1)}), bf16[4,32,2,2048]{3,0,2,1:T(4,128)(2,1)S(1)}, u32[]{:S(2)}, u32[]{:S(2)}) async-start(bf16[4,32,2,2048]{3,0,2,1:T(4,128)(2,1)} %copy.25), calls=%async_computation.1 | async-start | bytes 2097152 | tf_op jit(solution)/shard_map/all_to_all | solution.py:29
Sparse Core Ops, SparseCore 0:
  9.2 161.2 all-gather.2
where the time goes:
time: 237 us
  waiting for transfers between devices  170 us (72%)
  starting transfers between devices  21.2 us (9%)
  matrix products  17.3 us (7%)
  between operations  15.4 us (6%)
  local copies, waits for them, and re-layouts  9.66 us (4%)
  other arithmetic  3.06 us (1%)
    all_gather x1, waiting for transfers between devices, body(): lax.all_gather(my_integrals, 'blk', axis=1, tiled=True)  117 us
    all_to_all x1, waiting for transfers between devices, body(): lax.all_to_all(shaped, 'wide', split_axis=1, concat_axis=2, tiled=True)  28.2 us
    all_to_all x1, waiting for transfers between devices, body(): lax.all_to_all(ordered, 'wide', split_axis=2, concat_axis=1, tiled=True)  24.1 us
    dot_general x1, matrix products, body(): jnp.einsum('rc,kac->rka', pair_rows, lax.all_gather(my_integrals, 'blk',...  16 us
    all_to_all x1, starting transfers between devices, body(): lax.all_to_all(ordered, 'wide', split_axis=2, concat_axis=1, tiled=True)  11.3 us
    all_to_all x1, starting transfers between devices, body(): lax.all_to_all(shaped, 'wide', split_axis=1, concat_axis=2, tiled=True)  9.84 us
  transfers between devices with their start and end apart: 3, of which 3 were waited for; matrix products, arithmetic and copies ran while one was open for 4% of the time, Pallas kernels for 0%

commit v1 on v0

v1 whole, which is shorter than its diff:
```python
import jax
import jax.numpy as jnp
from jax import lax
from jax.sharding import PartitionSpec as P


def body(amplitudes, integrals, owner, targets, counts):
    wide_count = lax.axis_size("wide")
    blk_count = lax.axis_size("blk")
    my_index = lax.axis_index("wide")
    tile_ids = jnp.arange(owner.shape[0], dtype=jnp.int32)
    holder = jnp.sum(jnp.where(owner[None, :] == tile_ids[:, None], tile_ids[None, :], 0), axis=1)
    ni, _, nt, width = amplitudes.shape
    ordered = jnp.take(amplitudes.reshape(ni, nt, width).transpose(1, 0, 2), holder, axis=0)
    my_tile = lax.all_to_all(ordered, "wide", split_axis=0, concat_axis=0, tiled=True)
    rows = lax.all_gather(my_tile.reshape(wide_count * ni, width), "blk", axis=0, tiled=True)
    my_holder = lax.dynamic_index_in_dim(holder, my_index, 0, keepdims=False)
    my_count = lax.dynamic_index_in_dim(counts, my_holder, 0, keepdims=False)
    slot_ids = jnp.arange(targets.shape[1], dtype=jnp.int32)
    live_slots = (slot_ids < my_count).astype(jnp.float32)
    value = jnp.einsum("rc,kac->rka", rows, integrals[0], preferred_element_type=jnp.float32)
    shaped = (value * live_slots[None, :, None]).astype(jnp.bfloat16)
    nk, ab = shaped.shape[1:]
    shaped = shaped.reshape(blk_count, wide_count, ni, nk, ab).transpose(1, 0, 2, 3, 4)
    shaped = shaped.reshape(wide_count * blk_count, ni, nk, ab)
    received = lax.all_to_all(shaped, ("wide", "blk"), split_axis=0, concat_axis=0, tiled=True)
    received = received.reshape(wide_count, blk_count, ni, nk, ab)
    slot_targets = jnp.take(targets, holder, axis=0)
    window_ids = jnp.arange(wide_count, dtype=jnp.int32)
    selector = (slot_targets[None] == window_ids[:, None, None]).astype(jnp.bfloat16)
    ladder = jnp.einsum("pwk,wbika->piba", selector, received, preferred_element_type=jnp.float32)
    ladder = ladder.astype(jnp.bfloat16)
    return ladder.reshape(wide_count, ni, 1, blk_count * ab)


def solution(mesh):
    placed = (P("blk", "wide", None, None), P("wide", None, "blk", None), P(), P(), P())
    return jax.shard_map(
        body, mesh=mesh, in_specs=placed, out_specs=P(None, "blk", "wide", None), check_vma=False
    )
```

time: 237 us -> 167 us (0.70)
  waiting for transfers between devices: 170 us -> 74.8 us
  blocking collectives: 0 us -> 39.7 us
  starting transfers between devices: 21.2 us -> 12.7 us
  matrix products: 17.3 us -> 9.86 us
    all_gather x1, waiting for transfers between devices: 117 us -> 44.4 us  [body(): lax.all_gather(my_tile.reshape(wide_count * ni, width), 'blk', axis=0, ti...]
    all_to_all x0 -> x1, blocking collectives: none -> 39.7 us  [body(): lax.all_to_all(ordered, 'wide', split_axis=0, concat_axis=0, tiled=True)]
    all_to_all x2 -> x1, waiting for transfers between devices: 52.3 us -> 30.3 us  [body(): lax.all_to_all(shaped, ('wide', 'blk'), split_axis=0, concat_axis=0, tile...]
    all_to_all x2 -> x1, starting transfers between devices: 21.2 us -> 12.7 us  [body(): lax.all_to_all(shaped, ('wide', 'blk'), split_axis=0, concat_axis=0, tile...]
    dot_general x2, matrix products: 17.3 us -> 9.86 us  [the longest x1 9.09 us: body(): jnp.einsum('rc,kac->rka', rows, integrals[0], preferred_element_type=jnp....]
    reshape x1 -> x6, local copies, waits for them, and re-layouts: 1.79 us -> 5.55 us  [the longest x1 2.04 us: body(): shaped = shaped.reshape(wide_count * blk_count, ni, nk, ab)]
  transfers between devices with their start and end apart: 3 -> 2, of which waited for: 3 -> 2; matrix products, arithmetic and copies ran while one was open for 4% -> 2% of each run, Pallas kernels for 0% -> 0%
where the time goes in v1:
time: 167 us; the launch traced here: 166 us
  waiting for transfers between devices  74.8 us (45%)
  blocking collectives  39.7 us (24%)
  between operations  15.4 us (9%)
  starting transfers between devices  12.7 us (8%)
  local copies, waits for them, and re-layouts  11 us (7%)
  matrix products  9.86 us (6%)
  other arithmetic  2.08 us (1%)
    all_gather x1, waiting for transfers between devices, body(): lax.all_gather(my_tile.reshape(wide_count * ni, width), 'blk', axis=0, ti...  44.4 us
    all_to_all x1, blocking collectives, body(): lax.all_to_all(ordered, 'wide', split_axis=0, concat_axis=0, tiled=True)  39.7 us
    all_to_all x1, waiting for transfers between devices, body(): lax.all_to_all(shaped, ('wide', 'blk'), split_axis=0, concat_axis=0, tile...  30.3 us
    all_to_all x1, starting transfers between devices, body(): lax.all_to_all(shaped, ('wide', 'blk'), split_axis=0, concat_axis=0, tile...  12.7 us
    dot_general x1, matrix products, body(): jnp.einsum('rc,kac->rka', rows, integrals[0], preferred_element_type=jnp....  9.09 us
  transfers between devices with their start and end apart: 2, of which 2 were waited for; matrix products, arithmetic and copies ran while one was open for 2% of the time, Pallas kernels for 0%

profile of v1, /device:TPU:8, one launch (start us, length us, event | category | flops | bytes accessed | tf_op | source)
XLA Modules:
  0.0 165.6 jit_solution(17266843945001171867)
XLA Ops:
  6.5 0.0 all-gather.2.cloned.1.call-start
  6.5 0.8 select_reduce_fusion
  7.3 2.0 %copy.45 = bf16[4,1,32,4096]{3,0,2,1:T(4,128)(2,1)S(1)} copy(bf16[4,1,32,4096]{3,2,1,0:T(8,128)(2,1)} %param.5) | data formatting | bytes 2097152 | tf_op args[0]
  9.4 1.4 gather_fusion
  10.8 0.0 copy-start.1
  10.8 0.6 broadcast_select_fusion
  11.4 39.7 %all_to_all.10 = bf16[32,4,4096]{2,1,0:T(4,128)(2,1)S(1)} all-to-all(bf16[32,4,4096]{2,1,0:T(4,128)(2,1)S(1)} %broadcast_select_fusion), channel_id=1, replica_groups=mesh['wide'=32,'blk'=8] {'wide'}, dimensions={0} | all-to-all | bytes 2097152 | tf_op jit(solution)/shard_map/all_to_all | solution.py:15
  51.2 1.2 reshape.55
  52.3 0.0 all-gather.2.cloned.1.call-update
  52.3 0.6 dynamic_slice.7
  54.9 0.0 copy-done.1
  54.9 0.6 dynamic_slice.8
  55.5 0.6 compare_convert_fusion
  56.1 44.4 %all-gather.2.cloned.1.call-done = bf16[1024,4096]{1,0:T(8,128)(2,1)} async-done(((bf16[128,4096]{1,0:T(8,128)(2,1)}), bf16[1024,4096]{1,0:T(8,128)(2,1)}) %all-gather.2.cloned.1.call-update) | async-done | bytes 8388624 | tf_op jit(solution)/shard_map/all_gather | solution.py:16
  100.6 9.1 %multiply_convert_fusion = bf16[1024,2,256]{2,0,1:T(8,128)(2,1)S(1)} fusion(bf16[1,2,256,4096]{3,2,1,0:T(8,128)(2,1)} %param.6, bf16[1024,4096]{1,0:T(8,128)(2,1)} %all-gather.2.cloned.1.call-done, f32[2]{0:T(128)S(1)} %compare_convert_fusion), kind=kOutput, calls=%fused_computation.5 | convolution fusion | flops 4296015872 | bytes 13631496 | tf_op jit(solution)/shard_map/rc,kac->rka/dot_general | solution.py:21
  109.7 0.0 copy-start
  109.7 0.3 reshape.56
  110.0 0.6 copy.44
  110.6 2.0 %copy.27 = bf16[256,4,2,256]{3,2,1,0:T(2,128)(2,1)} copy(bf16[256,4,2,256]{3,0,2,1:T(8,128)(2,1)S(1)} %bitcast.46) | data formatting | bytes 2097152 | tf_op jit(solution)/shard_map/reshape | solution.py:25
  112.6 12.7 %all-to-all-start.1 = ((bf16[256,4,2,256]{3,2,1,0:T(2,128)(2,1)}), bf16[256,4,2,256]{3,2,1,0:T(2,128)(2,1)S(1)}, u32[]{:S(2)}, u32[]{:S(2)}) async-start(bf16[256,4,2,256]{3,2,1,0:T(2,128)(2,1)} %copy.27), calls=%async_computation.1 | async-start | bytes 2097152 | tf_op jit(solution)/shard_map/all_to_all | solution.py:26
  125.3 0.0 copy-done
  125.4 0.1 copy.29
  125.4 0.6 gather_fusion.1
  126.0 0.1 broadcast_select_fusion.1
  126.1 0.1 copy.30
  126.2 30.3 %all-to-all-done.1 = bf16[256,4,2,256]{3,2,1,0:T(2,128)(2,1)S(1)} async-done(((bf16[256,4,2,256]{3,2,1,0:T(2,128)(2,1)}), bf16[256,4,2,256]{3,2,1,0:T(2,128)(2,1)S(1)}, u32[]{:S(2)}, u32[]{:S(2)}) %all-to-all-start.1) | async-done | bytes 1048608 | tf_op jit(solution)/shard_map/all_to_all | solution.py:26
  156.5 0.8 fusion.8
  157.3 0.3 copy.38
  157.6 1.2 reshape.79
  (3 shorter events, 0.0 us)
Async XLA Ops:
  6.5 94.0 %all-gather.2.cloned.1.call-start = ((), (), s32[]{:S(2)}) async-start(), calls=%async_computation.2 | async-start | bytes 9437184 | tf_op jit(solution)/shard_map/all_gather | solution.py:16
  10.8 44.0 %copy-start.1 = (s32[32]{0:T(128)S(1)}, s32[32]{0:T(128)}, u32[]{:S(2)}) copy-start(s32[32]{0:T(128)} %param.9) | copy-start | bytes 388
  109.7 15.7 %copy-start = (s32[32,2]{0,1:T(2,128)S(1)}, s32[32,2]{0,1:T(2,128)}, u32[]{:S(2)}) copy-start(s32[32,2]{0,1:T(2,128)} %param.8) | copy-start | bytes 772
  112.6 43.9 %all-to-all-start.1 = ((bf16[256,4,2,256]{3,2,1,0:T(2,128)(2,1)}), bf16[256,4,2,256]{3,2,1,0:T(2,128)(2,1)S(1)}, u32[]{:S(2)}, u32[]{:S(2)}) async-start(bf16[256,4,2,256]{3,2,1,0:T(2,128)(2,1)} %copy.27), calls=%async_computation.1 | async-start | bytes 2097152 | tf_op jit(solution)/shard_map/all_to_all | solution.py:26
Sparse Core Ops, SparseCore 0:
  52.5 48.0 all-gather.1

commit v2 on v1

v2 whole, which is shorter than its diff:
```python
import functools
import jax
import jax.numpy as jnp
from jax import lax
from jax.experimental import pallas as pl
from jax.experimental.pallas import tpu as pltpu
from jax.sharding import PartitionSpec as P

MESH = pl.DeviceIdType.MESH
NX, NY, NZ = 4, 4, 8
NW = NX * NZ
NI = 4
ROWS = NW * NI
NT_DIMS = (((1,), (1,)), ((), ()))


def kernel(tab, amps, ints, out, stage, got, rows, held, made, back,
           arrive, from_up, from_down, far, home, local, sent, swap):
    w, b = lax.axis_index("wide"), lax.axis_index("blk")
    x, z = w // NZ, w % NZ
    y, c = b // 2, b % 2

    def wide_at(step, sign):
        dx, dz = step // NZ, step % NZ
        return ((x + NX + sign * dx) % NX) * NZ + (z + NZ + sign * dz) % NZ

    def blk_at(dy):
        return ((y + dy) % NY) * 2 + c

    def remote(src, dst, send, recv, device):
        return pltpu.make_async_remote_copy(
            src_ref=src, dst_ref=dst, send_sem=send, recv_sem=recv,
            device_id=device, device_id_type=MESH)

    partner = (w, y * 2 + 1 - c)

    barrier = pltpu.get_barrier_semaphore()
    pl.semaphore_signal(barrier, inc=1, device_id=partner, device_id_type=MESH)
    for dy in range(NY):
        @pl.loop(1 if dy == 0 else 0, NW)
        def _(step):
            pl.semaphore_signal(barrier, inc=1, device_id=(wide_at(step, 1), blk_at(dy)), device_id_type=MESH)

    own = pltpu.make_async_copy(ints, held.at[c], local.at[0])
    own.start()

    row = lax.broadcasted_iota(jnp.int32, (ROWS, ROWS), 0)
    col = lax.broadcasted_iota(jnp.int32, (ROWS, ROWS), 1)
    slot = jnp.broadcast_to(tab[2:3, :], (ROWS, ROWS))
    order = jnp.where((slot == row // NI) & (row % NI == col // NW), 1.0, 0.0).astype(jnp.bfloat16)
    width = amps.shape[2]
    for j in range(4):
        lanes = slice(j * width // 4, (j + 1) * width // 4)
        piece = amps[:, :, lanes].reshape(ROWS, width // 4)
        value = jnp.dot(order, piece, preferred_element_type=jnp.float32).astype(jnp.bfloat16)
        stage[:, :, lanes] = value.reshape(NW, NI, width // 4)

    pl.semaphore_wait(barrier, NW * NY)

    @pl.loop(1, NW)
    def _(step):
        to = wide_at(step, 1)
        remote(stage.at[to], got.at[0, step], sent.at[0], arrive.at[step], (to, b)).start()

    mine = pltpu.make_async_copy(stage.at[w], got.at[0, 0], arrive.at[0])
    mine.start()
    exchange = remote(ints, held.at[c], swap.at[0], swap.at[1], partner)
    exchange.start()

    up, down = (w, blk_at(1)), (w, blk_at(NY - 1))
    GROUP = 4

    def lay(part, group):
        first = pl.multiple_of(group * GROUP, GROUP)
        piece = got[part, pl.ds(first, GROUP)].reshape(GROUP * NI, width)
        rows[part, pl.ds(pl.multiple_of(group * GROUP * NI, GROUP * NI), GROUP * NI), :] = piece

    @pl.loop(0, NW // GROUP)
    def _(group):
        for j in range(GROUP):
            step = group * GROUP + j
            chunk = got.at[0, step]
            pltpu.make_async_copy(chunk, chunk, arrive.at[step]).wait()
            remote(chunk, got.at[3, step], sent.at[1], from_down.at[step], up).start()
            remote(chunk, got.at[1, step], sent.at[2], from_up.at[step], down).start()
        lay(0, group)

    own.wait()
    exchange.wait_recv()

    def contract(part):
        for cc in range(2):
            for k in range(2):
                value = lax.dot_general(rows[part], held[cc, k], NT_DIMS, preferred_element_type=jnp.float32)
                n = value.shape[1]
                lanes = slice((cc * 2 + k) * n, (cc * 2 + k + 1) * n)
                made[part, :, :, lanes] = value.astype(jnp.bfloat16).reshape(NW, NI, n)

    def give(part):
        to_blk = blk_at(part)

        @pl.loop(1 if part == 0 else 0, NW)
        def _(step):
            remote(made.at[part, step], back.at[y, w], sent.at[5], home.at[part], (wide_at(step, -1), to_blk)).start()

    contract(0)
    pltpu.make_async_copy(made.at[0, 0], back.at[y, w], home.at[0]).start()
    give(0)

    @pl.loop(0, NW // GROUP)
    def _(group):
        for j in range(GROUP):
            step = group * GROUP + j
            low, high = got.at[3, step], got.at[1, step]
            pltpu.make_async_copy(low, low, from_down.at[step]).wait()
            pltpu.make_async_copy(high, high, from_up.at[step]).wait()
            if j % 2 == 0:
                remote(low, got.at[2, step], sent.at[3], far.at[step], up).start()
            else:
                remote(high, got.at[2, step], sent.at[4], far.at[step], down).start()
        lay(3, group)
        lay(1, group)

    contract(3)
    give(3)
    contract(1)
    give(1)

    @pl.loop(0, NW // GROUP)
    def _(group):
        for j in range(GROUP):
            step = group * GROUP + j
            chunk = got.at[2, step]
            pltpu.make_async_copy(chunk, chunk, far.at[step]).wait()
        lay(2, group)

    contract(2)
    give(2)

    pick = []
    for k in range(2):
        target = jnp.broadcast_to(tab[k:k + 1, :], (ROWS, ROWS))
        pick.append(jnp.where((target == row // NI) & (row % NI == col % NI), 1.0, 0.0).astype(jnp.bfloat16))
    for part in (0, 3, 1, 2):
        origin = (y + NY - part) % NY
        block = back.at[origin]
        pltpu.make_async_copy(block, block, home.at[part]).wait()
        piece = back[origin].reshape(ROWS, back.shape[3])
        n = piece.shape[1] // 4
        for cc in range(2):
            total = jnp.dot(pick[0], piece[:, 2 * cc * n:(2 * cc + 1) * n], preferred_element_type=jnp.float32)
            total += jnp.dot(pick[1], piece[:, (2 * cc + 1) * n:(2 * cc + 2) * n], preferred_element_type=jnp.float32)
            lanes = pl.ds(pl.multiple_of((origin * 2 + cc) * n, n), n)
            out[:, :, lanes] = total.astype(jnp.bfloat16).reshape(NW, NI, n)

    def drain(ref, sem):
        pltpu.make_async_copy(ref, ref, sem).wait()

    drain(stage.at[pl.ds(0, NW - 1)], sent.at[0])
    drain(got.at[0], sent.at[1])
    drain(got.at[0], sent.at[2])
    drain(got.at[2, pl.ds(0, NW // 2)], sent.at[3])
    drain(got.at[2, pl.ds(0, NW // 2)], sent.at[4])
    for part in range(NY):
        if part:
            drain(made.at[part], sent.at[5])
        else:
            drain(made.at[part, pl.ds(0, NW - 1)], sent.at[5])
    exchange.wait_send()


def table(owner, targets, counts):
    shape = (8, ROWS, NW)
    r, m, q = (lax.broadcasted_iota(jnp.int32, shape, axis) for axis in range(3))
    second = jnp.where(counts > 1, targets[:, 1], -1)[None, None]
    first = jnp.where(counts > 0, targets[:, 0], -1)[None, None]
    target = jnp.where(r == 0, first, second)
    owners = owner[None, None]
    value = jnp.where(r < 2, jnp.where(owners == m // NI, target, 0), jnp.where(q == m % NW, owners, 0))
    return jnp.sum(value, axis=2)


def body(amplitudes, integrals, owner, targets, counts):
    amps, ints = amplitudes[:, 0], integrals[0]
    width = amps.shape[2]
    pairs = ints.shape[1]
    vmem = pl.BlockSpec(memory_space=pltpu.VMEM)
    dma = pltpu.SemaphoreType.DMA
    out = pl.pallas_call(
        kernel,
        out_shape=jax.ShapeDtypeStruct((NW, NI, 2 * NY * pairs), jnp.bfloat16),
        in_specs=[vmem, vmem, pl.BlockSpec(memory_space=pl.ANY)],
        out_specs=vmem,
        scratch_shapes=[
            pltpu.VMEM((NW, NI, width), jnp.bfloat16),
            pltpu.VMEM((NY, NW, NI, width), jnp.bfloat16),
            pltpu.VMEM((NY, ROWS, width), jnp.bfloat16),
            pltpu.VMEM((2, 2, pairs, width), jnp.bfloat16),
            pltpu.VMEM((NY, NW, NI, 4 * pairs), jnp.bfloat16),
            pltpu.VMEM((NY, NW, NI, 4 * pairs), jnp.bfloat16),
            dma((NW,)), dma((NW,)), dma((NW,)), dma((NW,)), dma((NY,)), dma((1,)), dma((6,)), dma((2,)),
        ],
        compiler_params=pltpu.CompilerParams(
            collective_id=0, has_side_effects=True, vmem_limit_bytes=48 << 20),
        name="ladder",
    )(table(owner, targets, counts), amps, ints)
    return out[:, :, None, :]


def solution(mesh):
    placed = (P("blk", "wide", None, None), P("wide", None, "blk", None), P(), P(), P())
    return jax.shard_map(
        body, mesh=mesh, in_specs=placed, out_specs=P(None, "blk", "wide", None), check_vma=False
    )
```

time: 167 us -> 80.6 us (0.48)
  waiting for transfers between devices: 74.8 us -> 0 us
  Pallas kernels: 0 us -> 74.6 us
  blocking collectives: 39.7 us -> 0 us
  between operations: 15.4 us -> 0.04 us
  starting transfers between devices: 12.7 us -> 0 us
  matrix products: 9.86 us -> 0 us
  local copies, waits for them, and re-layouts: 11 us -> 4.2 us
    pallas_call x0 -> x1, Pallas kernels: none -> 74.6 us  [body(): pl.pallas_call(kernel, out_shape=jax.ShapeDtypeStruct((NW, NI, 2 * NY * p...]
    all_gather x1 -> x0, waiting for transfers between devices: 44.4 us -> none  [body(): lax.all_gather(my_tile.reshape(wide_count * ni, width), 'blk', axis=0, ti...]
    all_to_all x1 -> x0, blocking collectives: 39.7 us -> none  [body(): lax.all_to_all(ordered, 'wide', split_axis=0, concat_axis=0, tiled=True)]
    all_to_all x1 -> x0, waiting for transfers between devices: 30.3 us -> none  [body(): lax.all_to_all(shaped, ('wide', 'blk'), split_axis=0, concat_axis=0, tile...]
    all_to_all x1 -> x0, starting transfers between devices: 12.7 us -> none  [body(): lax.all_to_all(shaped, ('wide', 'blk'), split_axis=0, concat_axis=0, tile...]
    dot_general x2 -> x0, matrix products: 9.86 us -> none  [the longest x1 9.09 us: body(): jnp.einsum('rc,kac->rka', rows, integrals[0], preferred_element_type=jnp....]
    reshape x6 -> x0, local copies, waits for them, and re-layouts: 5.55 us -> none  [the longest x1 2.04 us: body(): shaped = shaped.reshape(wide_count * blk_count, ni, nk, ab)]
    unnamed x6 -> x5, local copies, waits for them, and re-layouts: 2.14 us -> 4.2 us
  transfers between devices with their start and end apart: 2 -> 0, of which waited for: 2 -> 0; matrix products, arithmetic and copies ran while one was open for 2% -> 0% of each run, Pallas kernels for 0% -> 0%
where the time goes in v2:
time: 80.6 us; the launch traced here: 80.4 us
  Pallas kernels  74.6 us (93%)
  local copies, waits for them, and re-layouts  4.2 us (5%)
  other arithmetic  1.55 us (2%)
    pallas_call x1, Pallas kernels, body(): pl.pallas_call(kernel, out_shape=jax.ShapeDtypeStruct((NW, NI, 2 * NY * p...  74.6 us
    unnamed x5, local copies, waits for them, and re-layouts  4.2 us

profile of v2, /device:TPU:8, one launch (start us, length us, event | category | flops | bytes accessed | tf_op | source)
XLA Modules:
  0.0 80.4 jit_solution(2840437318726561973)
XLA Ops:
  0.0 0.8 compare_select_fusion.1
  0.8 0.8 select_reduce_fusion.tab
  1.6 0.0 copy-start
  1.6 2.2 %copy-done = bf16[1,2,256,4096]{3,2,1,0:T(8,128)(2,1)S(1)} copy-done((bf16[1,2,256,4096]{3,2,1,0:T(8,128)(2,1)S(1)}, bf16[1,2,256,4096]{3,2,1,0:T(8,128)(2,1)}, u32[]{:S(2)}) %copy-start) | copy-done | bytes 4194328
  3.8 0.0 copy-start.1
  3.8 1.2 %copy-done.1 = bf16[4,1,32,4096]{3,2,1,0:T(8,128)(2,1)S(1)} copy-done((bf16[4,1,32,4096]{3,2,1,0:T(8,128)(2,1)S(1)}, bf16[4,1,32,4096]{3,2,1,0:T(8,128)(2,1)}, u32[]{:S(2)}) %copy-start.1) | copy-done | bytes 1048600
  5.0 74.6 %ladder.1 = bf16[32,4,2048]{2,1,0:T(4,128)(2,1)S(1)} custom-call(s32[8,128]{1,0:T(8,128)S(1)} %select_reduce_fusion.tab, bf16[4,32,4096]{2,1,0:T(8,128)(2,1)S(1)} %bitcast.11, bf16[2,256,4096]{2,1,0:T(8,128)(2,1)S(1)} %bitcast.9), custom_call_target="tpu_custom_call" | custom-call | tf_op jit(solution)/shard_map/ladder/pallas_call | solution.py:189
  79.6 0.8 copy.9
  (4 shorter events, 0.0 us)
Async XLA Ops:
  1.6 2.2 %copy-start = (bf16[1,2,256,4096]{3,2,1,0:T(8,128)(2,1)S(1)}, bf16[1,2,256,4096]{3,2,1,0:T(8,128)(2,1)}, u32[]{:S(2)}) copy-start(bf16[1,2,256,4096]{3,2,1,0:T(8,128)(2,1)} %param.6) | copy-start | bytes 12582916
  3.8 1.2 %copy-start.1 = (bf16[4,1,32,4096]{3,2,1,0:T(8,128)(2,1)S(1)}, bf16[4,1,32,4096]{3,2,1,0:T(8,128)(2,1)}, u32[]{:S(2)}) copy-start(bf16[4,1,32,4096]{3,2,1,0:T(8,128)(2,1)} %param.5) | copy-start | bytes 3145732

commit v3 on v2

v3 whole, which is shorter than its diff:
```python
import functools
import jax
import jax.numpy as jnp
from jax import lax
from jax.experimental import pallas as pl
from jax.experimental.pallas import tpu as pltpu
from jax.sharding import PartitionSpec as P

MESH = pl.DeviceIdType.MESH
NX, NY, NZ = 4, 4, 8
NW = NX * NZ
NI = 4
ROWS = NW * NI
GROUP = 4
GROUPS = NW // GROUP
HALF = NW // 2
PLACE = (0, 2, 3, 1)
NT_DIMS = (((1,), (1,)), ((), ()))


def kernel(owner_hbm, targets_hbm, counts_hbm, amps_hbm, ints, out,
           owner, targets, counts, amps, stage, got, rows, held, made, back,
           arrive, from_up, from_down, far, home, local, sent, swap):
    w, b = lax.axis_index("wide"), lax.axis_index("blk")
    x, z = w // NZ, w % NZ
    y, c = b // 2, b % 2

    def offset(step):
        iz, ix = step // NX, step % NX
        dz = NZ // 2 + (iz + 1) // 2 * (1 - 2 * (iz % 2))
        dx = NX // 2 + (ix + 1) // 2 * (1 - 2 * (ix % 2))
        return dx, dz

    def wide_at(step, sign):
        dx, dz = offset(step)
        return ((x + NX + sign * dx) % NX) * NZ + (z + NZ + sign * dz) % NZ

    def blk_at(dy):
        return ((y + dy) % NY) * 2 + c

    def remote(src, dst, send, recv, device):
        return pltpu.make_async_remote_copy(
            src_ref=src, dst_ref=dst, send_sem=send, recv_sem=recv,
            device_id=device, device_id_type=MESH)

    def await_bytes(ref, sem):
        pltpu.make_async_copy(ref, ref, sem).wait()

    partner = (w, y * 2 + 1 - c)

    loads = [pltpu.make_async_copy(src, dst, local.at[n]) for n, (src, dst) in enumerate((
        (amps_hbm, amps), (owner_hbm, owner), (targets_hbm, targets), (counts_hbm, counts), (ints, held.at[c])))]
    for load in loads:
        load.start()

    barrier = pltpu.get_barrier_semaphore()
    pl.semaphore_signal(barrier, inc=1, device_id=partner, device_id_type=MESH)

    @pl.loop(0, NW - 1)
    def _(step):
        there = wide_at(step, 1)
        for dy in range(NY):
            pl.semaphore_signal(barrier, inc=1, device_id=(there, blk_at(dy)), device_id_type=MESH)

    for dy in range(1, NY):
        pl.semaphore_signal(barrier, inc=1, device_id=(w, blk_at(dy)), device_id_type=MESH)

    for load in loads[:4]:
        load.wait()
    row = lax.broadcasted_iota(jnp.int32, (ROWS, ROWS), 0)
    col = lax.broadcasted_iota(jnp.int32, (ROWS, ROWS), 1)
    same = row % NI == col // NW

    def spread(value):
        return jnp.broadcast_to(jnp.concatenate([value] * NI, axis=1), (ROWS, ROWS))

    def one_hot(value):
        return jnp.where((spread(value) == row // NI) & same, 1.0, 0.0).astype(jnp.bfloat16)

    order = one_hot(owner[...])
    width = amps.shape[2]
    for j in range(4):
        lanes = slice(j * width // 4, (j + 1) * width // 4)
        piece = amps[:, :, lanes].reshape(ROWS, width // 4)
        value = jnp.dot(order, piece, preferred_element_type=jnp.float32).astype(jnp.bfloat16)
        stage[:, :, lanes] = value.reshape(NW, NI, width // 4)

    pl.semaphore_wait(barrier, NW * NY)

    mine = pltpu.make_async_copy(stage.at[w], got.at[0, NW - 1], arrive.at[NW - 1])
    mine.start()

    @pl.loop(0, NW - 1)
    def _(step):
        to = wide_at(step, 1)
        remote(stage.at[to], got.at[0, step], sent.at[0], arrive.at[step], (to, b)).start()

    exchange = remote(ints, held.at[c], swap.at[0], swap.at[1], partner)
    exchange.start()

    pick = []
    for k in range(2):
        live = jnp.where(counts[...] > k, targets[k:k + 1, :], -1)
        chosen = lax.dot_general(one_hot(live), order, NT_DIMS, preferred_element_type=jnp.float32)
        pick.append(chosen.astype(jnp.bfloat16))

    up, down = (w, blk_at(1)), (w, blk_at(NY - 1))

    def lay(part, group):
        first = pl.multiple_of(group * GROUP, GROUP)
        piece = got[part, pl.ds(first, GROUP)].reshape(GROUP * NI, width)
        place = (group // 4 * NY + PLACE[part]) * 64 + group % 4 * 16
        rows[pl.ds(pl.multiple_of(place, 16), 16), :] = piece

    def forward(group):
        for j in range(GROUP):
            step = group * GROUP + j
            chunk = got.at[0, step]
            await_bytes(chunk, arrive.at[step])
            remote(chunk, got.at[3, step], sent.at[1], from_down.at[step], up).start()
            remote(chunk, got.at[1, step], sent.at[2], from_up.at[step], down).start()
        lay(0, group)

    def relay(group):
        for j in range(GROUP):
            step = group * GROUP + j
            low, high = got.at[3, step], got.at[1, step]
            await_bytes(low, from_down.at[step])
            await_bytes(high, from_up.at[step])
            if j % 2 == 0:
                remote(low, got.at[2, step], sent.at[3], far.at[step], up).start()
            else:
                remote(high, got.at[2, step], sent.at[4], far.at[step], down).start()
        lay(3, group)
        lay(1, group)

    def finish(group):
        for j in range(GROUP):
            step = group * GROUP + j
            await_bytes(got.at[2, step], far.at[step])
        lay(2, group)

    def contract(first, count):
        for cc in range(2):
            for k in range(2):
                value = lax.dot_general(rows[first * 64:(first + count) * 64, :], held[cc, k], NT_DIMS,
                                        preferred_element_type=jnp.float32)
                n = value.shape[1]
                lanes = slice((cc * 2 + k) * n, (cc * 2 + k + 1) * n)
                made[first * HALF:(first + count) * HALF, :, lanes] = value.astype(jnp.bfloat16).reshape(count * HALF, NI, n)

    def give(part, half):
        to_blk = blk_at(part)
        base = (half * NY + PLACE[part]) * HALF

        @pl.loop(0, HALF - 1 if part == 0 and half == 1 else HALF)
        def _(n):
            remote(made.at[base + n], back.at[y, w], sent.at[5], home.at[part],
                   (wide_at(half * HALF + n, -1), to_blk)).start()

        if part == 0 and half == 1:
            pltpu.make_async_copy(made.at[base + HALF - 1], back.at[y, w], home.at[0]).start()

    @pl.loop(0, 2)
    def _(group):
        forward(group)

    @pl.loop(2, 4)
    def _(group):
        forward(group)
        relay(group - 2)

    loads[4].wait()
    exchange.wait_recv()
    contract(0, 1)
    give(0, 0)

    @pl.loop(4, 6)
    def _(group):
        forward(group)
        relay(group - 2)
        finish(group - 4)

    contract(1, 2)
    give(3, 0)
    give(1, 0)

    @pl.loop(6, 8)
    def _(group):
        forward(group)
        relay(group - 2)
        finish(group - 4)

    contract(3, 2)
    give(2, 0)
    give(0, 1)

    @pl.loop(6, 8)
    def _(group):
        relay(group)

    contract(5, 2)
    give(3, 1)
    give(1, 1)

    @pl.loop(4, 8)
    def _(group):
        finish(group)

    contract(7, 1)
    give(2, 1)

    for part in (0, 3, 1, 2):
        origin = (y + NY - part) % NY
        await_bytes(back.at[origin], home.at[part])
        piece = back[origin].reshape(ROWS, back.shape[3])
        n = piece.shape[1] // 4
        for cc in range(2):
            total = jnp.dot(pick[0], piece[:, 2 * cc * n:(2 * cc + 1) * n], preferred_element_type=jnp.float32)
            total += jnp.dot(pick[1], piece[:, (2 * cc + 1) * n:(2 * cc + 2) * n], preferred_element_type=jnp.float32)
            lanes = pl.ds(pl.multiple_of((origin * 2 + cc) * n, n), n)
            out[:, :, lanes] = total.astype(jnp.bfloat16).reshape(NW, NI, n)

    await_bytes(stage.at[pl.ds(0, NW - 1)], sent.at[0])
    await_bytes(got.at[0], sent.at[1])
    await_bytes(got.at[0], sent.at[2])
    await_bytes(got.at[2, pl.ds(0, HALF)], sent.at[3])
    await_bytes(got.at[2, pl.ds(0, HALF)], sent.at[4])
    await_bytes(made.at[pl.ds(0, 8 * HALF - 1)], sent.at[5])
    exchange.wait_send()


def body(amplitudes, integrals, owner, targets, counts):
    amps, ints = amplitudes[:, 0], integrals[0]
    width = amps.shape[2]
    pairs = ints.shape[1]
    dma = pltpu.SemaphoreType.DMA
    out = pl.pallas_call(
        kernel,
        out_shape=jax.ShapeDtypeStruct((NW, NI, 2 * NY * pairs), jnp.bfloat16),
        in_specs=[pl.BlockSpec(memory_space=pl.ANY)] * 5,
        out_specs=pl.BlockSpec(memory_space=pltpu.VMEM),
        scratch_shapes=[
            pltpu.VMEM((1, NW), jnp.int32),
            pltpu.VMEM((2, NW), jnp.int32),
            pltpu.VMEM((1, NW), jnp.int32),
            pltpu.VMEM((NI, NW, width), jnp.bfloat16),
            pltpu.VMEM((NW, NI, width), jnp.bfloat16),
            pltpu.VMEM((NY, NW, NI, width), jnp.bfloat16),
            pltpu.VMEM((NY * ROWS, width), jnp.bfloat16),
            pltpu.VMEM((2, 2, pairs, width), jnp.bfloat16),
            pltpu.VMEM((NY * NW, NI, 4 * pairs), jnp.bfloat16),
            pltpu.VMEM((NY, NW, NI, 4 * pairs), jnp.bfloat16),
            dma((NW,)), dma((NW,)), dma((NW,)), dma((NW,)), dma((NY,)), dma((5,)), dma((6,)), dma((2,)),
        ],
        compiler_params=pltpu.CompilerParams(
            collective_id=0, has_side_effects=True, vmem_limit_bytes=60 << 20),
        name="ladder",
    )(owner[None], targets.T, counts[None], amps, ints)
    return out[:, :, None, :]


def solution(mesh):
    placed = (P("blk", "wide", None, None), P("wide", None, "blk", None), P(), P(), P())
    return jax.shard_map(
        body, mesh=mesh, in_specs=placed, out_specs=P(None, "blk", "wide", None), check_vma=False
    )
```

time: 80.6 us -> 81.8 us (1.015)
  Pallas kernels: 74.6 us -> 79.6 us
  local copies, waits for them, and re-layouts: 4.2 us -> 2.06 us
  other arithmetic: 1.55 us -> 0 us
    pallas_call x1, Pallas kernels: 74.6 us -> 79.6 us  [body(): pl.pallas_call(kernel, out_shape=jax.ShapeDtypeStruct((NW, NI, 2 * NY * p...]
    unnamed x5 -> x1, local copies, waits for them, and re-layouts: 4.2 us -> 2.06 us
where the time goes in v3:
time: 81.8 us; the launch traced here: 81.7 us
  Pallas kernels  79.6 us (97%)
  local copies, waits for them, and re-layouts  2.06 us (3%)
    pallas_call x1, Pallas kernels, body(): pl.pallas_call(kernel, out_shape=jax.ShapeDtypeStruct((NW, NI, 2 * NY * p...  79.6 us
    unnamed x1, local copies, waits for them, and re-layouts  2.06 us

profile of v3, /device:TPU:8, one launch (start us, length us, event | category | flops | bytes accessed | tf_op | source)
XLA Modules:
  0.0 81.7 jit_solution(2312679873657808682)
XLA Ops:
  0.0 79.6 %ladder.1 = bf16[32,4,2048]{2,1,0:T(4,128)(2,1)} custom-call(s32[1,32]{1,0:T(1,128)} %bitcast.12, s32[2,32]{1,0:T(2,128)} %bitcast.11, s32[1,32]{1,0:T(1,128)} %bitcast.13, bf16[4,32,4096]{2,1,0:T(8,128)(2,1)} %bitcast.10, bf16[2,256,4096]{2,1,0:T(8,128)(2,1)} %bitcast.8), custom_call_target="tpu_custom_call" | custom-call | tf_op jit(solution)/shard_map/ladder/pallas_call | solution.py:238
  79.6 2.1 %copy.8 = bf16[32,4,1,2048]{3,1,2,0:T(4,128)(2,1)} copy(bf16[32,4,1,2048]{3,1,2,0:T(4,128)(2,1)} %bitcast.9) | data formatting | bytes 1048576

commit v4 on v3

v4 whole, which is shorter than its diff:
```python
import functools
import jax
import jax.numpy as jnp
from jax import lax
from jax.experimental import pallas as pl
from jax.experimental.pallas import tpu as pltpu
from jax.sharding import PartitionSpec as P

MESH = pl.DeviceIdType.MESH
NX, NY, NZ = 4, 4, 8
NW = NX * NZ
NI = 4
ROWS = NW * NI
GROUP = 4
GROUPS = NW // GROUP
HALF = NW // 2
DZ = (0, 1, 7, 4, 3, 5, 2, 6)
PLACE = (0, 2, 3, 1)
NT_DIMS = (((1,), (1,)), ((), ()))


def kernel(owner_hbm, targets_hbm, counts_hbm, amps_hbm, ints, out,
           owner, targets, counts, amps, stage, got, rows, held, turned, made, back,
           arrive, from_up, from_down, far, home, local, sent, swap):
    w, b = lax.axis_index("wide"), lax.axis_index("blk")
    y, c = b // 2, b % 2
    xs = [lax.rem(w // NZ + d, NX) * NZ for d in range(NX)]
    zs = [lax.rem(w % NZ + d, NZ) for d in range(NZ)]
    blks = [lax.rem(y + d, NY) * 2 + c for d in range(NY)]

    def wide_at(step, sign):
        dz, dx = DZ[step // NX], step % NX
        return xs[sign * dx % NX] + zs[sign * dz % NZ]

    def remote(src, dst, send, recv, device):
        return pltpu.make_async_remote_copy(
            src_ref=src, dst_ref=dst, send_sem=send, recv_sem=recv,
            device_id=device, device_id_type=MESH)

    def await_bytes(ref, sem):
        pltpu.make_async_copy(ref, ref, sem).wait()

    partner = (w, y * 2 + 1 - c)

    loads = [pltpu.make_async_copy(src, dst, local.at[n]) for n, (src, dst) in enumerate((
        (amps_hbm, amps), (owner_hbm, owner), (targets_hbm, targets), (counts_hbm, counts), (ints, held.at[c])))]
    for load in loads:
        load.start()

    barrier = pltpu.get_barrier_semaphore()
    pl.semaphore_signal(barrier, inc=1, device_id=partner, device_id_type=MESH)
    for step in range(NW):
        for dy in range(NY):
            if step or dy:
                pl.semaphore_signal(barrier, inc=1, device_id=(wide_at(step, 1), blks[dy]), device_id_type=MESH)

    for load in loads[:4]:
        load.wait()
    row = lax.broadcasted_iota(jnp.int32, (ROWS, ROWS), 0)
    col = lax.broadcasted_iota(jnp.int32, (ROWS, ROWS), 1)
    same = row % NI == col // NW

    def spread(value):
        return jnp.broadcast_to(jnp.concatenate([value] * NI, axis=1), (ROWS, ROWS))

    def one_hot(value):
        return jnp.where((spread(value) == row // NI) & same, 1.0, 0.0).astype(jnp.bfloat16)

    order = one_hot(owner[...])
    width = amps.shape[2]
    for j in range(4):
        lanes = slice(j * width // 4, (j + 1) * width // 4)
        piece = amps[:, :, lanes].reshape(ROWS, width // 4)
        value = jnp.dot(order, piece, preferred_element_type=jnp.float32).astype(jnp.bfloat16)
        stage[:, :, lanes] = value.reshape(NW, NI, width // 4)

    pl.semaphore_wait(barrier, NW * NY)

    mine = pltpu.make_async_copy(stage.at[w], got.at[0, 0], arrive.at[0])
    mine.start()
    for step in range(1, NW):
        to = wide_at(step, 1)
        remote(stage.at[to], got.at[0, step], sent.at[0], arrive.at[step], (to, b)).start()

    exchange = remote(ints, held.at[c], swap.at[0], swap.at[1], partner)
    exchange.start()

    up, down = (w, blks[1]), (w, blks[NY - 1])
    pairs = held.shape[2]

    def lay(part, group):
        piece = got[part, group * GROUP:(group + 1) * GROUP].reshape(GROUP * NI, width)
        place = (group // 4 * NY + PLACE[part]) * 64 + group % 4 * 16
        rows[place:place + 16, :] = piece

    def forward(group):
        for step in range(group * GROUP, (group + 1) * GROUP):
            chunk = got.at[0, step]
            await_bytes(chunk, arrive.at[step])
            remote(chunk, got.at[3, step], sent.at[1], from_down.at[step], up).start()
            remote(chunk, got.at[1, step], sent.at[2], from_up.at[step], down).start()
        lay(0, group)

    def relay(group):
        for step in range(group * GROUP, (group + 1) * GROUP):
            low, high = got.at[3, step], got.at[1, step]
            await_bytes(low, from_down.at[step])
            await_bytes(high, from_up.at[step])
            if step % 2 == 0:
                remote(low, got.at[2, step], sent.at[3], far.at[step], up).start()
            else:
                remote(high, got.at[2, step], sent.at[4], far.at[step], down).start()
        lay(3, group)
        lay(1, group)

    def finish(group):
        for step in range(group * GROUP, (group + 1) * GROUP):
            await_bytes(got.at[2, step], far.at[step])
        lay(2, group)

    def turn(core, k):
        lanes = pl.ds(pl.multiple_of((core * 2 + k) * pairs, pairs), pairs)
        turned[:, lanes] = held[core, k].T

    def contract(first, count):
        for n in range(4):
            lanes = slice(n * pairs, (n + 1) * pairs)
            value = jnp.dot(rows[first * 64:(first + count) * 64, :], turned[:, lanes],
                            preferred_element_type=jnp.float32)
            made[first * HALF:(first + count) * HALF, :, lanes] = value.astype(jnp.bfloat16).reshape(count * HALF, NI, pairs)

    def give(part, half):
        base = (half * NY + PLACE[part]) * HALF
        for n in range(HALF):
            step = half * HALF + n
            if part == 0 and step == 0:
                pltpu.make_async_copy(made.at[base], back.at[y, w], home.at[0]).start()
            else:
                remote(made.at[base + n], back.at[y, w], sent.at[5], home.at[part],
                       (wide_at(step, -1), blks[part])).start()

    loads[4].wait()
    turn(c, 0)
    forward(0)
    turn(c, 1)
    forward(1)
    forward(2)
    relay(0)

    pick = []
    for k in range(2):
        live = jnp.where(counts[...] > k, targets[k:k + 1, :], -1)
        chosen = lax.dot_general(one_hot(live), order, NT_DIMS, preferred_element_type=jnp.float32)
        pick.append(chosen.astype(jnp.bfloat16))

    exchange.wait_recv()
    turn(1 - c, 0)
    forward(3)
    relay(1)
    turn(1 - c, 1)
    contract(0, 1)
    give(0, 0)
    forward(4)
    relay(2)
    finish(0)
    forward(5)
    relay(3)
    finish(1)
    contract(1, 2)
    give(3, 0)
    give(1, 0)
    forward(6)
    relay(4)
    finish(2)
    forward(7)
    relay(5)
    finish(3)
    contract(3, 2)
    give(2, 0)
    give(0, 1)
    relay(6)
    relay(7)
    contract(5, 2)
    give(3, 1)
    give(1, 1)
    for group in range(4, GROUPS):
        finish(group)
    contract(7, 1)
    give(2, 1)

    for part in (0, 3, 1, 2):
        origin = lax.rem(y + NY - part, NY)
        await_bytes(back.at[origin], home.at[part])
        piece = back[origin].reshape(ROWS, 4 * pairs)
        for cc in range(2):
            total = jnp.dot(pick[0], piece[:, 2 * cc * pairs:(2 * cc + 1) * pairs], preferred_element_type=jnp.float32)
            total += jnp.dot(pick[1], piece[:, (2 * cc + 1) * pairs:(2 * cc + 2) * pairs], preferred_element_type=jnp.float32)
            lanes = pl.ds(pl.multiple_of((origin * 2 + cc) * pairs, pairs), pairs)
            out[:, :, lanes] = total.astype(jnp.bfloat16).reshape(NW, NI, pairs)

    await_bytes(stage.at[pl.ds(0, NW - 1)], sent.at[0])
    await_bytes(got.at[0], sent.at[1])
    await_bytes(got.at[0], sent.at[2])
    await_bytes(got.at[2, pl.ds(0, HALF)], sent.at[3])
    await_bytes(got.at[2, pl.ds(0, HALF)], sent.at[4])
    await_bytes(made.at[pl.ds(0, 8 * HALF - 1)], sent.at[5])
    exchange.wait_send()


def body(amplitudes, integrals, owner, targets, counts):
    amps, ints = amplitudes[:, 0], integrals[0]
    width = amps.shape[2]
    pairs = ints.shape[1]
    dma = pltpu.SemaphoreType.DMA
    out = pl.pallas_call(
        kernel,
        out_shape=jax.ShapeDtypeStruct((NW, NI, 2 * NY * pairs), jnp.bfloat16),
        in_specs=[pl.BlockSpec(memory_space=pltpu.HBM)] * 5,
        out_specs=pl.BlockSpec(memory_space=pltpu.VMEM),
        scratch_shapes=[
            pltpu.VMEM((1, NW), jnp.int32),
            pltpu.VMEM((2, NW), jnp.int32),
            pltpu.VMEM((1, NW), jnp.int32),
            pltpu.VMEM((NI, NW, width), jnp.bfloat16),
            pltpu.VMEM((NW, NI, width), jnp.bfloat16),
            pltpu.VMEM((NY, NW, NI, width), jnp.bfloat16),
            pltpu.VMEM((NY * ROWS, width), jnp.bfloat16),
            pltpu.VMEM((2, 2, pairs, width), jnp.bfloat16),
            pltpu.VMEM((width, 4 * pairs), jnp.bfloat16),
            pltpu.VMEM((NY * NW, NI, 4 * pairs), jnp.bfloat16),
            pltpu.VMEM((NY, NW, NI, 4 * pairs), jnp.bfloat16),
            dma((NW,)), dma((NW,)), dma((NW,)), dma((NW,)), dma((NY,)), dma((5,)), dma((6,)), dma((2,)),
        ],
        compiler_params=pltpu.CompilerParams(
            collective_id=0, has_side_effects=True, vmem_limit_bytes=48 << 20),
        name="ladder",
    )(*(pltpu.with_memory_space_constraint(a, pltpu.HBM) for a in (owner[None], targets.T, counts[None], amps, ints)))
    return out[:, :, None, :]


def solution(mesh):
    placed = (P("blk", "wide", None, None), P("wide", None, "blk", None), P(), P(), P())
    return jax.shard_map(
        body, mesh=mesh, in_specs=placed, out_specs=P(None, "blk", "wide", None), check_vma=False
    )
```

time: 81.8 us -> 71.8 us (0.88)
  Pallas kernels: 79.6 us -> 70.9 us
  local copies, waits for them, and re-layouts: 2.06 us -> 0.8 us
    pallas_call x1, Pallas kernels: 79.6 us -> 70.9 us  [body(): pl.pallas_call(kernel, out_shape=jax.ShapeDtypeStruct((NW, NI, 2 * NY * p...]
    unnamed x1, local copies, waits for them, and re-layouts: 2.06 us -> 0.8 us
where the time goes in v4:
time: 71.8 us
  Pallas kernels  70.9 us (99%)
  local copies, waits for them, and re-layouts  0.8 us (1%)
    pallas_call x1, Pallas kernels, body(): pl.pallas_call(kernel, out_shape=jax.ShapeDtypeStruct((NW, NI, 2 * NY * p...  70.9 us

profile of v4, /device:TPU:8, one launch (start us, length us, event | category | flops | bytes accessed | tf_op | source)
XLA Modules:
  0.0 71.8 jit_solution(16513792600045988537)
XLA Ops:
  0.0 70.9 %ladder.1 = bf16[32,4,2048]{2,1,0:T(4,128)(2,1)S(1)} custom-call(s32[1,32]{1,0:T(1,128)} %bitcast.12, s32[2,32]{1,0:T(2,128)} %bitcast.11, s32[1,32]{1,0:T(1,128)} %bitcast.13, bf16[4,32,4096]{2,1,0:T(8,128)(2,1)} %bitcast.10, bf16[2,256,4096]{2,1,0:T(8,128)(2,1)} %bitcast.9), custom_call_target="tpu_custom_call" | custom-call | tf_op jit(solution)/shard_map/ladder/pallas_call | solution.py:215
  71.0 0.8 %copy.8 = bf16[32,4,1,2048]{3,1,2,0:T(4,128)(2,1)} copy(bf16[32,4,1,2048]{3,1,2,0:T(4,128)(2,1)S(1)} %bitcast.8) | data formatting | bytes 1048576

commit v5 on v4

--- a/solution.py
+++ b/solution.py
@@ -20,8 +20,8 @@
 
 
 def kernel(owner_hbm, targets_hbm, counts_hbm, amps_hbm, ints, out,
-           owner, targets, counts, amps, stage, got, rows, held, turned, made, back,
-           arrive, from_up, from_down, far, home, local, sent, swap):
+           owner, targets, counts, amps, stage, got, rows, held, turned, made, back, summed, final,
+           arrive, from_up, from_down, far, home, last, local, sent, swap):
     w, b = lax.axis_index("wide"), lax.axis_index("blk")
     y, c = b // 2, b % 2
     xs = [lax.rem(w // NZ + d, NX) * NZ for d in range(NX)]
@@ -49,10 +49,10 @@
 
     barrier = pltpu.get_barrier_semaphore()
     pl.semaphore_signal(barrier, inc=1, device_id=partner, device_id_type=MESH)
-    for step in range(NW):
-        for dy in range(NY):
-            if step or dy:
-                pl.semaphore_signal(barrier, inc=1, device_id=(wide_at(step, 1), blks[dy]), device_id_type=MESH)
+    for dy in range(1, NY):
+        pl.semaphore_signal(barrier, inc=1, device_id=(w, blks[dy]), device_id_type=MESH)
+    for step in range(1, NW):
+        pl.semaphore_signal(barrier, inc=1, device_id=(wide_at(step, 1), b), device_id_type=MESH)
 
     for load in loads[:4]:
         load.wait()
@@ -74,7 +74,7 @@
         value = jnp.dot(order, piece, preferred_element_type=jnp.float32).astype(jnp.bfloat16)
         stage[:, :, lanes] = value.reshape(NW, NI, width // 4)
 
-    pl.semaphore_wait(barrier, NW * NY)
+    pl.semaphore_wait(barrier, NW + NY - 1)
 
     mine = pltpu.make_async_copy(stage.at[w], got.at[0, 0], arrive.at[0])
     mine.start()
@@ -122,22 +122,41 @@
         lanes = pl.ds(pl.multiple_of((core * 2 + k) * pairs, pairs), pairs)
         turned[:, lanes] = held[core, k].T
 
-    def contract(first, count):
+    def contract(first, count, spare=0):
         for n in range(4):
             lanes = slice(n * pairs, (n + 1) * pairs)
-            value = jnp.dot(rows[first * 64:(first + count) * 64, :], turned[:, lanes],
-                            preferred_element_type=jnp.float32)
+            value = jnp.dot(rows[(first - spare) * 64:(first + count) * 64, :], turned[:, lanes],
+                            preferred_element_type=jnp.float32)[spare * 64:]
             made[first * HALF:(first + count) * HALF, :, lanes] = value.astype(jnp.bfloat16).reshape(count * HALF, NI, pairs)
 
     def give(part, half):
         base = (half * NY + PLACE[part]) * HALF
         for n in range(HALF):
             step = half * HALF + n
-            if part == 0 and step == 0:
-                pltpu.make_async_copy(made.at[base], back.at[y, w], home.at[0]).start()
+            if step == 0:
+                pltpu.make_async_copy(made.at[base], back.at[part, w], home.at[part]).start()
             else:
-                remote(made.at[base + n], back.at[y, w], sent.at[5], home.at[part],
-                       (wide_at(step, -1), blks[part])).start()
+                remote(made.at[base + n], back.at[part, w], sent.at[5], home.at[part],
+                       (wide_at(step, -1), b)).start()
+
+    def sumup(part):
+        await_bytes(back.at[part], home.at[part])
+        piece = back[part].reshape(ROWS, 4 * pairs)
+        for cc in range(2):
+            total = jnp.dot(pick[0], piece[:, 2 * cc * pairs:(2 * cc + 1) * pairs], preferred_element_type=jnp.float32)
+            total += jnp.dot(pick[1], piece[:, (2 * cc + 1) * pairs:(2 * cc + 2) * pairs], preferred_element_type=jnp.float32)
+            total = total.astype(jnp.bfloat16).reshape(NW, NI, pairs)
+            if part == 0:
+                out[:, :, pl.ds(pl.multiple_of((y * 2 + cc) * pairs, pairs), pairs)] = total
+            else:
+                summed[part, :, :, cc * pairs:(cc + 1) * pairs] = total
+        if part:
+            remote(summed.at[part], final.at[part], sent.at[6], last.at[part], (w, blks[part])).start()
+
+    def settle(part):
+        await_bytes(final.at[part], last.at[part])
+        origin = lax.rem(y + NY - part, NY)
+        out[:, :, pl.ds(pl.multiple_of(origin * 2 * pairs, 2 * pairs), 2 * pairs)] = final[part]
 
     loads[4].wait()
     turn(c, 0)
@@ -185,25 +204,24 @@
     give(1, 1)
     for group in range(4, GROUPS):
         finish(group)
-    contract(7, 1)
+    contract(7, 1, 1)
     give(2, 1)
 
-    for part in (0, 3, 1, 2):
-        origin = lax.rem(y + NY - part, NY)
-        await_bytes(back.at[origin], home.at[part])
-        piece = back[origin].reshape(ROWS, 4 * pairs)
-        for cc in range(2):
-            total = jnp.dot(pick[0], piece[:, 2 * cc * pairs:(2 * cc + 1) * pairs], preferred_element_type=jnp.float32)
-            total += jnp.dot(pick[1], piece[:, (2 * cc + 1) * pairs:(2 * cc + 2) * pairs], preferred_element_type=jnp.float32)
-            lanes = pl.ds(pl.multiple_of((origin * 2 + cc) * pairs, pairs), pairs)
-            out[:, :, lanes] = total.astype(jnp.bfloat16).reshape(NW, NI, pairs)
+    sumup(0)
+    sumup(3)
+    sumup(1)
+    sumup(2)
+    settle(3)
+    settle(1)
+    settle(2)
 
     await_bytes(stage.at[pl.ds(0, NW - 1)], sent.at[0])
     await_bytes(got.at[0], sent.at[1])
     await_bytes(got.at[0], sent.at[2])
     await_bytes(got.at[2, pl.ds(0, HALF)], sent.at[3])
     await_bytes(got.at[2, pl.ds(0, HALF)], sent.at[4])
-    await_bytes(made.at[pl.ds(0, 8 * HALF - 1)], sent.at[5])
+    await_bytes(made.at[pl.ds(0, NY * (NW - 1))], sent.at[5])
+    await_bytes(summed.at[pl.ds(0, NY - 1)], sent.at[6])
     exchange.wait_send()
 
 
@@ -229,7 +247,9 @@
             pltpu.VMEM((width, 4 * pairs), jnp.bfloat16),
             pltpu.VMEM((NY * NW, NI, 4 * pairs), jnp.bfloat16),
             pltpu.VMEM((NY, NW, NI, 4 * pairs), jnp.bfloat16),
-            dma((NW,)), dma((NW,)), dma((NW,)), dma((NW,)), dma((NY,)), dma((5,)), dma((6,)), dma((2,)),
+            pltpu.VMEM((NY, NW, NI, 2 * pairs), jnp.bfloat16),
+            pltpu.VMEM((NY, NW, NI, 2 * pairs), jnp.bfloat16),
+            dma((NW,)), dma((NW,)), dma((NW,)), dma((NW,)), dma((NY,)), dma((NY,)), dma((5,)), dma((7,)), dma((2,)),
         ],
         compiler_params=pltpu.CompilerParams(
             collective_id=0, has_side_effects=True, vmem_limit_bytes=48 << 20),

time: 71.8 us -> 67.6 us (0.942); the launches traced: 71.8 us -> 66.7 us
  Pallas kernels: 70.9 us -> 65.9 us
    pallas_call x1, Pallas kernels: 70.9 us -> 65.9 us  [body(): pl.pallas_call(kernel, out_shape=jax.ShapeDtypeStruct((NW, NI, 2 * NY * p...]
where the time goes in v5:
time: 67.6 us; the launch traced here: 66.7 us
  Pallas kernels  65.9 us (97%)
  local copies, waits for them, and re-layouts  0.8 us (1%)
    pallas_call x1, Pallas kernels, body(): pl.pallas_call(kernel, out_shape=jax.ShapeDtypeStruct((NW, NI, 2 * NY * p...  65.9 us

profile of v5, /device:TPU:8, one launch (start us, length us, event | category | flops | bytes accessed | tf_op | source)
XLA Modules:
  0.0 66.7 jit_solution(8273017196687960510)
XLA Ops:
  0.0 65.9 %ladder.1 = bf16[32,4,2048]{2,1,0:T(4,128)(2,1)S(1)} custom-call(s32[1,32]{1,0:T(1,128)} %bitcast.12, s32[2,32]{1,0:T(2,128)} %bitcast.11, s32[1,32]{1,0:T(1,128)} %bitcast.13, bf16[4,32,4096]{2,1,0:T(8,128)(2,1)} %bitcast.10, bf16[2,256,4096]{2,1,0:T(8,128)(2,1)} %bitcast.9), custom_call_target="tpu_custom_call" | custom-call | tf_op jit(solution)/shard_map/ladder/pallas_call | solution.py:233
  65.9 0.8 %copy.8 = bf16[32,4,1,2048]{3,1,2,0:T(4,128)(2,1)} copy(bf16[32,4,1,2048]{3,1,2,0:T(4,128)(2,1)S(1)} %bitcast.8) | data formatting | bytes 1048576

commit v6 on v5

--- a/solution.py
+++ b/solution.py
@@ -13,9 +13,13 @@
 ROWS = NW * NI
 GROUP = 4
 GROUPS = NW // GROUP
-HALF = NW // 2
 DZ = (0, 1, 7, 4, 3, 5, 2, 6)
-PLACE = (0, 2, 3, 1)
+BLOCKS = ((0, 0, 4), (3, 0, 4), (1, 0, 4), (0, 4, 6), (0, 6, 8), (3, 4, 6), (1, 4, 6), (2, 0, 4),
+          (3, 6, 8), (1, 6, 8), (2, 4, 6), (2, 6, 8))
+SLOT = {}
+for _part, _first, _end in BLOCKS:
+    for _group in range(_first, _end):
+        SLOT[_part, _group] = len(SLOT)
 NT_DIMS = (((1,), (1,)), ((), ()))
 
 
@@ -49,10 +53,12 @@
 
     barrier = pltpu.get_barrier_semaphore()
     pl.semaphore_signal(barrier, inc=1, device_id=partner, device_id_type=MESH)
-    for dy in range(1, NY):
+    for dy in (1, 3):
         pl.semaphore_signal(barrier, inc=1, device_id=(w, blks[dy]), device_id_type=MESH)
-    for step in range(1, NW):
-        pl.semaphore_signal(barrier, inc=1, device_id=(wide_at(step, 1), b), device_id_type=MESH)
+    for step in range(NW):
+        for dy in (0, 2):
+            if step or dy:
+                pl.semaphore_signal(barrier, inc=1, device_id=(wide_at(step, 1), blks[dy]), device_id_type=MESH)
 
     for load in loads[:4]:
         load.wait()
@@ -74,7 +80,7 @@
         value = jnp.dot(order, piece, preferred_element_type=jnp.float32).astype(jnp.bfloat16)
         stage[:, :, lanes] = value.reshape(NW, NI, width // 4)
 
-    pl.semaphore_wait(barrier, NW + NY - 1)
+    pl.semaphore_wait(barrier, 2 * NW + 2)
 
     mine = pltpu.make_async_copy(stage.at[w], got.at[0, 0], arrive.at[0])
     mine.start()
@@ -90,8 +96,8 @@
 
     def lay(part, group):
         piece = got[part, group * GROUP:(group + 1) * GROUP].reshape(GROUP * NI, width)
-        place = (group // 4 * NY + PLACE[part]) * 64 + group % 4 * 16
-        rows[place:place + 16, :] = piece
+        place = SLOT[part, group] * GROUP * NI
+        rows[place:place + GROUP * NI, :] = piece
 
     def forward(group):
         for step in range(group * GROUP, (group + 1) * GROUP):
@@ -122,22 +128,21 @@
         lanes = pl.ds(pl.multiple_of((core * 2 + k) * pairs, pairs), pairs)
         turned[:, lanes] = held[core, k].T
 
-    def contract(first, count, spare=0):
+    def contract(first, end, spare=0):
         for n in range(4):
             lanes = slice(n * pairs, (n + 1) * pairs)
-            value = jnp.dot(rows[(first - spare) * 64:(first + count) * 64, :], turned[:, lanes],
-                            preferred_element_type=jnp.float32)[spare * 64:]
-            made[first * HALF:(first + count) * HALF, :, lanes] = value.astype(jnp.bfloat16).reshape(count * HALF, NI, pairs)
-
-    def give(part, half):
-        base = (half * NY + PLACE[part]) * HALF
-        for n in range(HALF):
-            step = half * HALF + n
-            if step == 0:
-                pltpu.make_async_copy(made.at[base], back.at[part, w], home.at[part]).start()
+            value = jnp.dot(rows[first - spare:end, :], turned[:, lanes], preferred_element_type=jnp.float32)[spare:]
+            made[first // NI:end // NI, :, lanes] = value.astype(jnp.bfloat16).reshape((end - first) // NI, NI, pairs)
+
+    def give(part, first, end):
+        for step in range(first * GROUP, end * GROUP):
+            chunk = made.at[SLOT[part, step // GROUP] * GROUP + step % GROUP]
+            if part == 2:
+                remote(chunk, back.at[part, w], sent.at[5], home.at[part], (wide_at(step, -1), blks[2])).start()
+            elif step == 0:
+                pltpu.make_async_copy(chunk, back.at[part, w], home.at[part]).start()
             else:
-                remote(made.at[base + n], back.at[part, w], sent.at[5], home.at[part],
-                       (wide_at(step, -1), b)).start()
+                remote(chunk, back.at[part, w], sent.at[5], home.at[part], (wide_at(step, -1), b)).start()
 
     def sumup(part):
         await_bytes(back.at[part], home.at[part])
@@ -146,11 +151,12 @@
             total = jnp.dot(pick[0], piece[:, 2 * cc * pairs:(2 * cc + 1) * pairs], preferred_element_type=jnp.float32)
             total += jnp.dot(pick[1], piece[:, (2 * cc + 1) * pairs:(2 * cc + 2) * pairs], preferred_element_type=jnp.float32)
             total = total.astype(jnp.bfloat16).reshape(NW, NI, pairs)
-            if part == 0:
-                out[:, :, pl.ds(pl.multiple_of((y * 2 + cc) * pairs, pairs), pairs)] = total
+            if part % 2 == 0:
+                origin = lax.rem(y + part, NY)
+                out[:, :, pl.ds(pl.multiple_of((origin * 2 + cc) * pairs, pairs), pairs)] = total
             else:
                 summed[part, :, :, cc * pairs:(cc + 1) * pairs] = total
-        if part:
+        if part % 2:
             remote(summed.at[part], final.at[part], sent.at[6], last.at[part], (w, blks[part])).start()
 
     def settle(part):
@@ -177,51 +183,56 @@
     forward(3)
     relay(1)
     turn(1 - c, 1)
-    contract(0, 1)
-    give(0, 0)
+    contract(0, 64)
+    give(0, 0, 4)
     forward(4)
     relay(2)
     finish(0)
     forward(5)
     relay(3)
     finish(1)
-    contract(1, 2)
-    give(3, 0)
-    give(1, 0)
+    contract(64, 224)
+    give(3, 0, 4)
+    give(1, 0, 4)
+    give(0, 4, 6)
     forward(6)
     relay(4)
     finish(2)
     forward(7)
     relay(5)
     finish(3)
-    contract(3, 2)
-    give(2, 0)
-    give(0, 1)
+    contract(224, 384)
+    give(3, 4, 6)
+    give(1, 4, 6)
+    give(0, 6, 8)
     relay(6)
     relay(7)
-    contract(5, 2)
-    give(3, 1)
-    give(1, 1)
-    for group in range(4, GROUPS):
-        finish(group)
-    contract(7, 1, 1)
-    give(2, 1)
-
-    sumup(0)
+    give(2, 0, 4)
+    finish(4)
+    finish(5)
+    contract(384, 480, 32)
+    give(3, 6, 8)
+    give(1, 6, 8)
+    give(2, 4, 6)
+    finish(6)
+    finish(7)
+    contract(480, 512, 96)
+    give(2, 6, 8)
+
     sumup(3)
     sumup(1)
+    sumup(0)
     sumup(2)
     settle(3)
     settle(1)
-    settle(2)
 
     await_bytes(stage.at[pl.ds(0, NW - 1)], sent.at[0])
     await_bytes(got.at[0], sent.at[1])
     await_bytes(got.at[0], sent.at[2])
-    await_bytes(got.at[2, pl.ds(0, HALF)], sent.at[3])
-    await_bytes(got.at[2, pl.ds(0, HALF)], sent.at[4])
-    await_bytes(made.at[pl.ds(0, NY * (NW - 1))], sent.at[5])
-    await_bytes(summed.at[pl.ds(0, NY - 1)], sent.at[6])
+    await_bytes(got.at[2, pl.ds(0, NW // 2)], sent.at[3])
+    await_bytes(got.at[2, pl.ds(0, NW // 2)], sent.at[4])
+    await_bytes(made.at[pl.ds(0, NY * NW - 3)], sent.at[5])
+    await_bytes(summed.at[pl.ds(0, 2)], sent.at[6])
     exchange.wait_send()
 
 

time: 67.6 us -> 66.6 us (0.985)
  Pallas kernels: 65.9 us -> 65.1 us
    pallas_call x1, Pallas kernels: 65.9 us -> 65.1 us  [body(): pl.pallas_call(kernel, out_shape=jax.ShapeDtypeStruct((NW, NI, 2 * NY * p...]
where the time goes in v6:
time: 66.6 us; the launch traced here: 65.9 us
  Pallas kernels  65.1 us (98%)
  local copies, waits for them, and re-layouts  0.8 us (1%)
    pallas_call x1, Pallas kernels, body(): pl.pallas_call(kernel, out_shape=jax.ShapeDtypeStruct((NW, NI, 2 * NY * p...  65.1 us

profile of v6, /device:TPU:8, one launch (start us, length us, event | category | flops | bytes accessed | tf_op | source)
XLA Modules:
  0.0 65.9 jit_solution(15822882187882044774)
XLA Ops:
  0.0 65.1 %ladder.1 = bf16[32,4,2048]{2,1,0:T(4,128)(2,1)S(1)} custom-call(s32[1,32]{1,0:T(1,128)} %bitcast.12, s32[2,32]{1,0:T(2,128)} %bitcast.11, s32[1,32]{1,0:T(1,128)} %bitcast.13, bf16[4,32,4096]{2,1,0:T(8,128)(2,1)} %bitcast.10, bf16[2,256,4096]{2,1,0:T(8,128)(2,1)} %bitcast.9), custom_call_target="tpu_custom_call" | custom-call | tf_op jit(solution)/shard_map/ladder/pallas_call | solution.py:244
  65.1 0.8 %copy.8 = bf16[32,4,1,2048]{3,1,2,0:T(4,128)(2,1)} copy(bf16[32,4,1,2048]{3,1,2,0:T(4,128)(2,1)S(1)} %bitcast.8) | data formatting | bytes 1048576

commit v7 on v6

--- a/solution.py
+++ b/solution.py
@@ -12,8 +12,10 @@
 NI = 4
 ROWS = NW * NI
 GROUP = 4
+PIECES = 4
 GROUPS = NW // GROUP
-DZ = (0, 1, 7, 4, 3, 5, 2, 6)
+ORDER = ((0, 0), (1, 0), (3, 0), (0, 1), (0, 7), (2, 0), (1, 1), (3, 1), (1, 7), (3, 7), (2, 1), (2, 7)) + tuple(
+    (dx, dz) for dz in (4, 3, 5, 2, 6) for dx in range(4))
 BLOCKS = ((0, 0, 4), (3, 0, 4), (1, 0, 4), (0, 4, 6), (0, 6, 8), (3, 4, 6), (1, 4, 6), (2, 0, 4),
           (3, 6, 8), (1, 6, 8), (2, 4, 6), (2, 6, 8))
 SLOT = {}
@@ -33,7 +35,7 @@
     blks = [lax.rem(y + d, NY) * 2 + c for d in range(NY)]
 
     def wide_at(step, sign):
-        dz, dx = DZ[step // NX], step % NX
+        dx, dz = ORDER[step]
         return xs[sign * dx % NX] + zs[sign * dz % NZ]
 
     def remote(src, dst, send, recv, device):
@@ -86,7 +88,9 @@
     mine.start()
     for step in range(1, NW):
         to = wide_at(step, 1)
-        remote(stage.at[to], got.at[0, step], sent.at[0], arrive.at[step], (to, b)).start()
+        for n in range(PIECES):
+            lanes = pl.ds(n * (width // PIECES), width // PIECES)
+            remote(stage.at[to, :, lanes], got.at[0, step, :, lanes], sent.at[0], arrive.at[step], (to, b)).start()
 
     exchange = remote(ints, held.at[c], swap.at[0], swap.at[1], partner)
     exchange.start()
@@ -128,21 +132,22 @@
         lanes = pl.ds(pl.multiple_of((core * 2 + k) * pairs, pairs), pairs)
         turned[:, lanes] = held[core, k].T
 
-    def contract(first, end, spare=0):
-        for n in range(4):
-            lanes = slice(n * pairs, (n + 1) * pairs)
-            value = jnp.dot(rows[first - spare:end, :], turned[:, lanes], preferred_element_type=jnp.float32)[spare:]
-            made[first // NI:end // NI, :, lanes] = value.astype(jnp.bfloat16).reshape((end - first) // NI, NI, pairs)
-
-    def give(part, first, end):
+    def contract(first, end, spare=0, lanes=(0, 1, 2, 3)):
+        for n in lanes:
+            cols = slice(n * pairs, (n + 1) * pairs)
+            value = jnp.dot(rows[first - spare:end, :], turned[:, cols], preferred_element_type=jnp.float32)[spare:]
+            made[first // NI:end // NI, :, cols] = value.astype(jnp.bfloat16).reshape((end - first) // NI, NI, pairs)
+
+    def give(part, first, end, lanes=slice(None)):
         for step in range(first * GROUP, end * GROUP):
-            chunk = made.at[SLOT[part, step // GROUP] * GROUP + step % GROUP]
+            chunk = made.at[SLOT[part, step // GROUP] * GROUP + step % GROUP, :, lanes]
+            there = back.at[part, w, :, lanes]
             if part == 2:
-                remote(chunk, back.at[part, w], sent.at[5], home.at[part], (wide_at(step, -1), blks[2])).start()
+                remote(chunk, there, sent.at[5], home.at[part], (wide_at(step, -1), blks[2])).start()
             elif step == 0:
-                pltpu.make_async_copy(chunk, back.at[part, w], home.at[part]).start()
+                pltpu.make_async_copy(chunk, there, home.at[part]).start()
             else:
-                remote(chunk, back.at[part, w], sent.at[5], home.at[part], (wide_at(step, -1), b)).start()
+                remote(chunk, there, sent.at[5], home.at[part], (wide_at(step, -1), b)).start()
 
     def sumup(part):
         await_bytes(back.at[part], home.at[part])
@@ -164,11 +169,11 @@
         origin = lax.rem(y + NY - part, NY)
         out[:, :, pl.ds(pl.multiple_of(origin * 2 * pairs, 2 * pairs), 2 * pairs)] = final[part]
 
+    forward(0)
     loads[4].wait()
     turn(c, 0)
-    forward(0)
+    forward(1)
     turn(c, 1)
-    forward(1)
     forward(2)
     relay(0)
 
@@ -216,8 +221,9 @@
     give(2, 4, 6)
     finish(6)
     finish(7)
-    contract(480, 512, 96)
-    give(2, 6, 8)
+    for cc in range(2):
+        contract(480, 512, 96, (2 * cc, 2 * cc + 1))
+        give(2, 6, 8, pl.ds(2 * cc * pairs, 2 * pairs))
 
     sumup(3)
     sumup(1)

time: 66.6 us -> 65.2 us (0.979)
  Pallas kernels: 65.1 us -> 64 us
    pallas_call x1, Pallas kernels: 65.1 us -> 64 us  [body(): pl.pallas_call(kernel, out_shape=jax.ShapeDtypeStruct((NW, NI, 2 * NY * p...]
where the time goes in v7:
time: 65.2 us; the launch traced here: 64.8 us
  Pallas kernels  64 us (98%)
  local copies, waits for them, and re-layouts  0.8 us (1%)
    pallas_call x1, Pallas kernels, body(): pl.pallas_call(kernel, out_shape=jax.ShapeDtypeStruct((NW, NI, 2 * NY * p...  64 us

profile of v7, /device:TPU:8, one launch (start us, length us, event | category | flops | bytes accessed | tf_op | source)
XLA Modules:
  0.0 64.8 jit_solution(9857615231988212041)
XLA Ops:
  0.0 64.0 %ladder.1 = bf16[32,4,2048]{2,1,0:T(4,128)(2,1)S(1)} custom-call(s32[1,32]{1,0:T(1,128)} %bitcast.12, s32[2,32]{1,0:T(2,128)} %bitcast.11, s32[1,32]{1,0:T(1,128)} %bitcast.13, bf16[4,32,4096]{2,1,0:T(8,128)(2,1)} %bitcast.10, bf16[2,256,4096]{2,1,0:T(8,128)(2,1)} %bitcast.9), custom_call_target="tpu_custom_call" | custom-call | tf_op jit(solution)/shard_map/ladder/pallas_call | solution.py:250
  64.0 0.8 %copy.8 = bf16[32,4,1,2048]{3,1,2,0:T(4,128)(2,1)} copy(bf16[32,4,1,2048]{3,1,2,0:T(4,128)(2,1)S(1)} %bitcast.8) | data formatting | bytes 1048576

commit v8 on v7

--- a/solution.py
+++ b/solution.py
@@ -212,12 +212,13 @@
     give(0, 6, 8)
     relay(6)
     relay(7)
+    contract(384, 448, 64)
+    give(3, 6, 8)
+    give(1, 6, 8)
     give(2, 0, 4)
     finish(4)
     finish(5)
-    contract(384, 480, 32)
-    give(3, 6, 8)
-    give(1, 6, 8)
+    contract(448, 480, 96)
     give(2, 4, 6)
     finish(6)
     finish(7)

time: 65.2 us -> 64.3 us (0.986)
  Pallas kernels: 64 us -> 63 us
    pallas_call x1, Pallas kernels: 64 us -> 63 us  [body(): pl.pallas_call(kernel, out_shape=jax.ShapeDtypeStruct((NW, NI, 2 * NY * p...]
where the time goes in v8:
time: 64.3 us; the launch traced here: 63.8 us
  Pallas kernels  63 us (98%)
  local copies, waits for them, and re-layouts  0.8 us (1%)
    pallas_call x1, Pallas kernels, body(): pl.pallas_call(kernel, out_shape=jax.ShapeDtypeStruct((NW, NI, 2 * NY * p...  63 us

profile of v8, /device:TPU:8, one launch (start us, length us, event | category | flops | bytes accessed | tf_op | source)
XLA Modules:
  0.0 63.8 jit_solution(7950604007993644540)
XLA Ops:
  0.0 63.0 %ladder.1 = bf16[32,4,2048]{2,1,0:T(4,128)(2,1)S(1)} custom-call(s32[1,32]{1,0:T(1,128)} %bitcast.12, s32[2,32]{1,0:T(2,128)} %bitcast.11, s32[1,32]{1,0:T(1,128)} %bitcast.13, bf16[4,32,4096]{2,1,0:T(8,128)(2,1)} %bitcast.10, bf16[2,256,4096]{2,1,0:T(8,128)(2,1)} %bitcast.9), custom_call_target="tpu_custom_call" | custom-call | tf_op jit(solution)/shard_map/ladder/pallas_call | solution.py:251
  63.0 0.8 %copy.8 = bf16[32,4,1,2048]{3,1,2,0:T(4,128)(2,1)} copy(bf16[32,4,1,2048]{3,1,2,0:T(4,128)(2,1)S(1)} %bitcast.8) | data formatting | bytes 1048576
